TPU v7x, 32 devices: a whole 2x2x4 slice. The times are simulated.
32 devices in a mesh: pair: 2 (over core), lat: 4 (over y, x), tok: 4 (over z).
Axes of the slice: x: 2, y: 2, z: 4, core: 2. Of those that a mesh axis runs over, the one named last changes fastest.
Arguments:
- residual: bfloat16 [2, 512, 4096], P('pair', 'tok', 'lat'), may hold values from -6 to 6
- matches: int32 [2, 512], P('pair', 'tok'), may hold values from 0 to 511, as said below
- kl_grad: bfloat16 [512, 4096], P('tok', 'lat'), may hold values from -6 to 6
- active_blocks: int32 [64, 2], replicated, may hold values from 0 to 31, all different within a row; in each aligned block of 16 rows (0 to 15, 16 to 31, ...) at most 2 rows name the same one
- encoder: bfloat16 [4096, 4096], P(None, ('pair', 'lat', 'tok')), may hold values from -0.09375 to 0.09375
- encoder_offset_bias: float32 [4096], P(('pair', 'lat', 'tok')), may hold values from -3 to 3
- decoder: bfloat16 [4096, 4096], P(('pair', 'lat', 'tok')), may hold values from -0.5 to 0.5
- dec_bias: float32 [4096], P('lat'), may hold values from -3 to 3
Outputs:
- reconstruction: bfloat16 [512, 4096], P('tok', 'lat')
- scores: float32 [4096], P(('pair', 'lat', 'tok'))
Inputs may be any that keep to these rules, and one draw needn't show every extreme that they name: For each model m and matched token k: k - 128 < matches[m, k] <= k (at least 0); where k is a positive multiple of 128, matches[m, k] = k - 127. `active_blocks`: each row lists 2 different latent blocks. Among the 16 rows of one tok index (aligned blocks of rows) no latent block is listed more than 2 times, and some latent block is listed exactly 2 times.
All inputs are finite; a program needn't handle non-finite values.
Results may differ from a plain program's by a relative error of at most 0.0085.
Values may be sent and summed in bfloat16 or wider, within the bound.
A program may use at most 64 MiB of HBM per device.

v0:
```python
import math
import jax
import jax.numpy as jnp
from jax import lax
from jax.sharding import PartitionSpec as P

TBLK = 8
MOST = 2


def passed_along(x, axis, by):
    devices = lax.axis_size(axis)
    pairs = [(i, i + by) for i in range(devices) if 0 <= i + by < devices]
    return lax.ppermute(x, axis, pairs)


def from_partner(x, axis, bit):
    return lax.ppermute(x, axis, [(i, i ^ 1 << bit) for i in range(lax.axis_size(axis))])


def slot_table(my_lists, targets, slot_ids):
    listed = jnp.any(my_lists[:, :, None] == targets[None, None, :], axis=1).astype(jnp.int32)
    ranking = jnp.cumsum(listed, axis=0) - listed
    return (listed.T[:, None, :] * (ranking.T[:, None, :] == slot_ids[None, :, None])).astype(
        jnp.bfloat16
    )


def shards(
    residual, matches, kl_grad, active_blocks, encoder, encoder_offset_bias, decoder, dec_bias
):
    tok_dev = residual.shape[1]
    tok_count = lax.axis_size("tok")
    lat_count = lax.axis_size("lat")
    tok_here = lax.axis_index("tok")
    own_rows = residual[0]
    earlier = passed_along(own_rows, "tok", 1)
    window = jnp.concatenate([earlier, own_rows], axis=0)
    first_row = (tok_here - 1) * tok_dev
    local_index = matches[0] - first_row
    matched = jnp.take(window, local_index, axis=0)
    partner = from_partner(matched, "pair", 0)
    is_chat = lax.axis_index("pair") == 1
    chat_rows = jnp.where(is_chat, matched, partner)
    base_rows = jnp.where(is_chat, partner, matched)
    delta_rows = (chat_rows.astype(jnp.float32) - base_rows.astype(jnp.float32)).astype(
        jnp.bfloat16
    )
    tb_dev = tok_dev // TBLK
    pair_base = lax.axis_index("pair") * lat_count
    row_base = (pair_base + lax.axis_index("lat")) * tok_count
    my_block = row_base + tok_here
    my_lists = lax.dynamic_slice_in_dim(active_blocks, tok_here * tb_dev, tb_dev, 0)
    slot_ids = jnp.arange(MOST, dtype=jnp.int32)
    targets = row_base + jnp.arange(tok_count, dtype=jnp.int32)
    chooser = slot_table(my_lists, targets, slot_ids)
    mine_listed = jnp.any(active_blocks == my_block, axis=1).astype(jnp.int32)
    counts = jnp.sum(mine_listed.reshape(tok_count, tb_dev), axis=1)
    padded_output = (slot_ids[None, :] < counts[:, None]).astype(jnp.float32)[:, :, None, None]

    def select_slots(blocks):
        return jnp.einsum(
            "ksb,btd->kstd", chooser, blocks, preferred_element_type=jnp.float32
        ).astype(jnp.bfloat16)

    full_delta, full_grad = (
        lax.all_gather(delta_rows, "lat", axis=1, tiled=True),
        lax.all_gather(kl_grad, "lat", axis=1, tiled=True),
    )
    full_width = full_delta.shape[1]
    sent_delta = select_slots(full_delta.reshape(tb_dev, TBLK, full_width))
    sent_grad = select_slots(full_grad.reshape(tb_dev, TBLK, full_width))
    got_delta, got_grad = (
        lax.all_to_all(sent_delta, "tok", split_axis=0, concat_axis=0, tiled=True),
        lax.all_to_all(sent_grad, "tok", split_axis=0, concat_axis=0, tiled=True),
    )
    preactivation = jnp.einsum(
        "kstd,dc->kstc", got_delta, encoder, preferred_element_type=jnp.float32
    )
    gradient_inner_product = jnp.einsum(
        "kstd,cd->kstc", got_grad, decoder, preferred_element_type=jnp.float32
    )
    activation_value = jnp.maximum(preactivation + encoder_offset_bias, 0.0) * padded_output
    every_token_rows = tok_dev * tok_count
    scores = jnp.sum(activation_value * gradient_inner_product, axis=(0, 1, 2)) / math.sqrt(
        every_token_rows / 8
    )
    activation_half_precision = activation_value.astype(jnp.bfloat16)
    pieces_out = jnp.einsum(
        "fazg,gh->fazh", activation_half_precision, decoder, preferred_element_type=jnp.float32
    ).astype(jnp.bfloat16)
    returned = lax.all_to_all(pieces_out, "tok", split_axis=0, concat_axis=0, tiled=True)
    source_sums = jnp.einsum(
        "ksb,kstd->btd", chooser, returned, preferred_element_type=jnp.float32
    ).reshape(tok_dev, -1)
    shared = lax.psum_scatter(
        source_sums.astype(jnp.bfloat16), "lat", scatter_dimension=1, tiled=True
    )
    summed = lax.psum(shared, "pair").astype(jnp.float32)
    return ((summed + dec_bias).astype(jnp.bfloat16), scores)


def solution(mesh):
    placed = (
        P("pair", "tok", "lat"),
        P("pair", "tok"),
        P("tok", "lat"),
        P(),
        P(None, ("pair", "lat", "tok")),
        P(("pair", "lat", "tok")),
        P(("pair", "lat", "tok"), None),
        P("lat"),
    )
    return jax.shard_map(
        shards,
        mesh=mesh,
        in_specs=placed,
        out_specs=(P("tok", "lat"), P(("pair", "lat", "tok"))),
        check_vma=False,
    )
```

profile of v0, /device:TPU:0, one launch (start us, length us, event | category | flops | bytes accessed | tf_op | source)
XLA Modules:
  0.0 148.8 jit_solution(7111867988648437557)
XLA Ops:
  7.2 5.1 %collective-permute-start = (bf16[128,1024]{1,0:T(8,128)(2,1)}, bf16[128,1024]{1,0:T(8,128)(2,1)S(1)}, u32[]{:S(2)}, u32[]{:S(2)}) collective-permute-start(bf16[128,1024]{1,0:T(8,128)(2,1)} %bitcast.56), channel_id=1, source_target_pairs={{0,1},{1,2},{2,3},{4,5},{5,6},{6,7},{8,9},{9,10},{10,11},{12,13},{... | collective-permute-start | bytes 786440 | tf_op jit(solution)/shard_map/ppermute | solution.py:14
  12.3 0.7 fusion.20
  13.0 0.7 compare_and_fusion
  13.7 4.5 %collective-permute-done = bf16[128,1024]{1,0:T(8,128)(2,1)S(1)} collective-permute-done((bf16[128,1024]{1,0:T(8,128)(2,1)}, bf16[128,1024]{1,0:T(8,128)(2,1)S(1)}, u32[]{:S(2)}, u32[]{:S(2)}) %collective-permute-start) | collective-permute-done | bytes 262176 | tf_op jit(solution)/shard_map/ppermute | solution.py:14
  18.2 1.0 pad_maximum_fusion
  19.2 0.9 gather_fusion
  20.0 0.1 broadcast_select_fusion
  20.2 1.5 %collective-permute-done.1 = bf16[128,1024]{1,0:T(8,128)(2,1)S(1)} collective-permute-done((bf16[128,1024]{1,0:T(8,128)(2,1)S(1)}, bf16[128,1024]{1,0:T(8,128)(2,1)S(1)}, u32[]{:S(2)}, u32[]{:S(2)}) %collective-permute-start.1) | collective-permute-done | bytes 262176 | tf_op jit(solution)/shard_map/ppermute | solution.py:18
  21.7 0.9 subtract_convert_fusion
  22.8 0.1 compare_reduce_fusion
  22.9 0.1 copy.48
  23.2 28.2 %all-gather.3.cloned.1.call-done = bf16[128,4096]{1,0:T(8,128)(2,1)} async-done(((bf16[128,1024]{1,0:T(8,128)(2,1)}), bf16[128,4096]{1,0:T(8,128)(2,1)}) %all-gather.3.cloned.1.call-update) | async-done | bytes 1048592 | tf_op jit(solution)/shard_map/all_gather | solution.py:67
  51.4 2.5 %convolution_convert_fusion.1 = bf16[4,2,8,4096]{3,0,2,1:T(4,128)(2,1)S(1)} fusion(bf16[16,8,4096]{2,1,0:T(8,128)(2,1)} %bitcast.54, s32[4,16]{1,0:T(4,128)S(1)} %copy.50, s32[4,16]{1,0:T(4,128)S(1)} %copy.49), kind=kOutput, calls=%fused_computation.4 | convolution fusion | flops 8651136 | bytes 1573376 | tf_op jit(solution)/shard_map/ksb,btd->kstd/dot_general | solution.py:62
  53.9 1.1 copy.52
  55.0 4.6 %all-to-all-start = ((bf16[4,2,8,4096]{3,2,1,0:T(8,128)(2,1)}), bf16[4,2,8,4096]{3,2,1,0:T(8,128)(2,1)S(1)}, u32[]{:S(2)}, u32[]{:S(2)}) async-start(bf16[4,2,8,4096]{3,2,1,0:T(8,128)(2,1)} %copy.52), calls=%async_computation | async-start | bytes 1048576 | tf_op jit(solution)/shard_map/all_to_all | solution.py:74
  59.6 0.7 all-gather.5.cloned.1.call-update
  60.5 0.1 reduce_sum.18
  60.7 13.2 %all-to-all-done = bf16[4,2,8,4096]{3,2,1,0:T(8,128)(2,1)S(1)} async-done(((bf16[4,2,8,4096]{3,2,1,0:T(8,128)(2,1)}), bf16[4,2,8,4096]{3,2,1,0:T(8,128)(2,1)S(1)}, u32[]{:S(2)}, u32[]{:S(2)}) %all-to-all-start) | async-done | bytes 524320 | tf_op jit(solution)/shard_map/all_to_all | solution.py:74
  73.9 0.3 fusion.25
  74.2 0.3 convolution_convert_fusion.2
  74.5 0.5 copy.54
  75.1 16.4 %all_to_all.15 = bf16[4,2,8,4096]{3,1,2,0:T(2,128)(2,1)S(1)} all-to-all(bf16[4,2,8,4096]{3,1,2,0:T(2,128)(2,1)S(1)} %copy.54), channel_id=1, replica_groups=mesh['pair'=2,'lat'=4,'tok'=4] {'tok'}, dimensions={0} | all-to-all | bytes 1048576 | tf_op jit(solution)/shard_map/all_to_all | solution.py:92
  91.5 0.7 fusion
  92.2 1.6 %copy.76 = bf16[16,8,4096]{2,1,0:T(8,128)(2,1)} copy(bf16[16,8,4096]{2,0,1:T(8,128)(2,1)S(1)} %fusion) | data formatting | bytes 2097152 | tf_op jit(solution)/shard_map/convert_element_type | solution.py:97
  93.9 2.5 %convolution_convert_fusion = bf16[4,2,8,4096]{3,0,2,1:T(4,128)(2,1)S(1)} fusion(bf16[16,8,4096]{2,1,0:T(8,128)(2,1)} %bitcast.55, s32[4,16]{1,0:T(4,128)S(1)} %copy.50, s32[4,16]{1,0:T(4,128)S(1)} %copy.49), kind=kOutput, calls=%fused_computation.3 | convolution fusion | flops 8651136 | bytes 1573376 | tf_op jit(solution)/shard_map/ksb,btd->kstd/dot_general | solution.py:62
  96.3 1.1 copy.58
  97.4 3.5 %all-to-all-start.2 = ((bf16[4,2,8,4096]{3,2,1,0:T(8,128)(2,1)}), bf16[4,2,8,4096]{3,2,1,0:T(8,128)(2,1)S(1)}, u32[]{:S(2)}, u32[]{:S(2)}) async-start(bf16[4,2,8,4096]{3,2,1,0:T(8,128)(2,1)} %copy.58), calls=%async_computation.3 | async-start | bytes 1048576 | tf_op jit(solution)/shard_map/all_to_all | solution.py:75
  101.0 19.1 %reduce-scatter.2.cloned.1.call-done = bf16[128,1024]{1,0:T(8,128)(2,1)} async-done(((bf16[128,4096]{1,0:T(8,128)(2,1)}), bf16[128,1024]{1,0:T(8,128)(2,1)}) %reduce-scatter.2.cloned.1.call-update) | async-done | bytes 262160 | tf_op jit(solution)/shard_map/reduce_scatter | solution.py:96
  120.1 0.5 fusion.3
  120.6 0.5 broadcast_multiply_fusion
  121.1 19.4 %all-reduce.2.cloned.1.call-done = bf16[128,1024]{1,0:T(8,128)(2,1)} async-done(((bf16[128,1024]{1,0:T(8,128)(2,1)}), bf16[128,1024]{1,0:T(8,128)(2,1)}) %all-reduce.2.cloned.1.call-update) | async-done | bytes 262160 | tf_op jit(solution)/shard_map/psum | solution.py:99
  140.5 1.7 %add_convert_fusion = bf16[128,1024]{1,0:T(8,128)(2,1)} fusion(bf16[128,1024]{1,0:T(8,128)(2,1)} %all-reduce.2.cloned.1.call-done, f32[1024]{0:T(1024)S(1)} %copy-done.2), kind=kLoop, calls=%fused_computation.21 | loop fusion | flops 393216 | bytes 528384 | tf_op jit(solution)/shard_map/convert_element_type | solution.py:100
  (32 shorter events, 0.8 us)
Async XLA Ops:
  7.2 67.0 %copy-start = (bf16[128,4096]{1,0:T(8,128)(2,1)S(1)}, bf16[128,4096]{1,0:T(8,128)(2,1)}, u32[]{:S(2)}) copy-start(bf16[128,4096]{1,0:T(8,128)(2,1)} %param.14) | copy-start | bytes 3145732
  7.2 44.2 %all-gather.3.cloned.1.call-start = ((), (), s32[]{:S(2)}) async-start(), calls=%async_computation.4 | async-start | bytes 1310720 | tf_op jit(solution)/shard_map/all_gather | solution.py:67
  7.2 11.0 %collective-permute-start = (bf16[128,1024]{1,0:T(8,128)(2,1)}, bf16[128,1024]{1,0:T(8,128)(2,1)S(1)}, u32[]{:S(2)}, u32[]{:S(2)}) collective-permute-start(bf16[128,1024]{1,0:T(8,128)(2,1)} %bitcast.56), channel_id=1, source_target_pairs={{0,1},{1,2},{2,3},{4,5},{5,6},{6,7},{8,9},{9,10},{10,11},{12,13},{... | collective-permute-start | bytes 786440 | tf_op jit(solution)/shard_map/ppermute | solution.py:14
  20.0 2.7 %copy-start.3 = (s32[64,2]{0,1:T(2,128)S(1)}, s32[64,2]{0,1:T(2,128)}, u32[]{:S(2)}) copy-start(s32[64,2]{0,1:T(2,128)} %param.11) | copy-start | bytes 1540
  20.1 1.6 %collective-permute-start.1 = (bf16[128,1024]{1,0:T(8,128)(2,1)S(1)}, bf16[128,1024]{1,0:T(8,128)(2,1)S(1)}, u32[]{:S(2)}, u32[]{:S(2)}) collective-permute-start(bf16[128,1024]{1,0:T(8,128)(2,1)S(1)} %broadcast_select_fusion), channel_id=1, source_target_pairs={{0,16},{16,0},{1,17},{17,1},{2,18},{18,2},{3,19},{19,3},{4,20},{20... | collective-permute-start | bytes 786440 | tf_op jit(solution)/shard_map/ppermute | solution.py:18
  53.8 20.1 %copy-start.1 = (bf16[4096,128]{1,0:T(8,128)(2,1)S(1)}, bf16[4096,128]{1,0:T(8,128)(2,1)}, u32[]{:S(2)}) copy-start(bf16[4096,128]{1,0:T(8,128)(2,1)} %param.12) | copy-start | bytes 3145732
  53.9 20.0 %copy-start.4 = (f32[128]{0:T(128)S(1)}, f32[128]{0:T(128)}, u32[]{:S(2)}) copy-start(f32[128]{0:T(128)} %param.13) | copy-start | bytes 1540
  55.0 18.9 %all-to-all-start = ((bf16[4,2,8,4096]{3,2,1,0:T(8,128)(2,1)}), bf16[4,2,8,4096]{3,2,1,0:T(8,128)(2,1)S(1)}, u32[]{:S(2)}, u32[]{:S(2)}) async-start(bf16[4,2,8,4096]{3,2,1,0:T(8,128)(2,1)} %copy.52), calls=%async_computation | async-start | bytes 1048576 | tf_op jit(solution)/shard_map/all_to_all | solution.py:74
  59.6 34.3 %all-gather.5.cloned.1.call-start = ((), (), s32[]{:S(2)}) async-start(), calls=%async_computation.7 | async-start | bytes 1310720 | tf_op jit(solution)/shard_map/all_gather | solution.py:68
  60.3 59.8 %reduce-scatter.2.cloned.1.call-start = ((), (), s32[]{:S(2)}) async-start(), calls=%async_computation.5 | async-start | bytes 1310720 | tf_op jit(solution)/shard_map/reduce_scatter | solution.py:96
  97.4 22.7 %all-to-all-start.2 = ((bf16[4,2,8,4096]{3,2,1,0:T(8,128)(2,1)}), bf16[4,2,8,4096]{3,2,1,0:T(8,128)(2,1)S(1)}, u32[]{:S(2)}, u32[]{:S(2)}) async-start(bf16[4,2,8,4096]{3,2,1,0:T(8,128)(2,1)} %copy.58), calls=%async_computation.3 | async-start | bytes 1048576 | tf_op jit(solution)/shard_map/all_to_all | solution.py:75
  100.9 39.6 %copy-start.2 = (f32[1024]{0:T(1024)S(1)}, f32[1024]{0:T(1024)}, u32[]{:S(2)}) copy-start(f32[1024]{0:T(1024)} %param.15) | copy-start | bytes 12292
  100.9 39.6 %all-reduce.2.cloned.1.call-start = ((), (), s32[]{:S(2)}) async-start(), calls=%async_computation.6 | async-start | bytes 524288 | tf_op jit(solution)/shard_map/psum | solution.py:99
Sparse Core Ops, SparseCore 0:
  22.8 28.5 all-gather.2
  62.2 26.9 all-gather.4
  94.0 26.0 reduce-scatter.1
  122.3 18.2 all-reduce.1
where the time goes:
time: 149 us
  waiting for transfers between devices  86.7 us (58%)
  blocking collectives  16.4 us (11%)
  between operations  13.9 us (9%)
  starting transfers between devices  13.4 us (9%)
  matrix products  6.75 us (5%)
  other arithmetic  5.9 us (4%)
  local copies, waits for them, and re-layouts  5.64 us (4%)
    all_gather x1, waiting for transfers between devices, shards(): lax.all_gather(delta_rows, 'lat', axis=1, tiled=True)  28.2 us
    psum x1, waiting for transfers between devices, shards(): summed = lax.psum(shared, 'pair').astype(jnp.float32)  19.4 us
    reduce_scatter x1, waiting for transfers between devices, shards(): lax.psum_scatter(source_sums.astype(jnp.bfloat16), 'lat', scatter_dimensi...  19.1 us
    all_to_all x1, blocking collectives, shards(): lax.all_to_all(pieces_out, 'tok', split_axis=0, concat_axis=0, tiled=True)  16.4 us
    all_to_all x1, waiting for transfers between devices, shards(): lax.all_to_all(sent_delta, 'tok', split_axis=0, concat_axis=0, tiled=True)  13.2 us
    ppermute x1, starting transfers between devices, passed_along(): return lax.ppermute(x, axis, pairs)  5.11 us
    dot_general x2, matrix products, select_slots(): jnp.einsum('ksb,btd->kstd', chooser, blocks, preferred_element_type=jnp.f...  4.93 us
    all_to_all x1, starting transfers between devices, shards(): lax.all_to_all(sent_delta, 'tok', split_axis=0, concat_axis=0, tiled=True)  4.6 us
  transfers between devices with their start and end apart: 8, of which 6 were waited for; matrix products, arithmetic and copies ran while one was open for 7% of the time, Pallas kernels for 0%

commit v1 on v0

--- a/solution.py
+++ b/solution.py
@@ -29,6 +29,31 @@
 def shards(
     residual, matches, kl_grad, active_blocks, encoder, encoder_offset_bias, decoder, dec_bias
 ):
+
+    def _meet_clusters(panel):
+        link_axis = "lat"
+        block_out, val2, y1 = (lax.axis_size(link_axis), lax.axis_index(link_axis), panel.shape[1])
+        pages = tuple((h * block_out if j == 1 else h for j, h in enumerate(panel.shape)))
+        back = lax.dynamic_update_slice_in_dim(
+            jnp.zeros(pages, panel.dtype), panel, val2 * y1, axis=1
+        )
+        upper = spare = panel
+        for dev_i in tuple(range(1, block_out // 2 + 1)):
+            upper = lax.ppermute(
+                upper, link_axis, tuple(((j, (j + 1) % block_out) for j in range(block_out)))
+            )
+            back = lax.dynamic_update_slice_in_dim(
+                back, upper, (val2 - dev_i) % block_out * y1, axis=1
+            )
+            if 2 * dev_i < block_out:
+                spare = lax.ppermute(
+                    spare, link_axis, tuple(((j, (j - 1) % block_out) for j in range(block_out)))
+                )
+                back = lax.dynamic_update_slice_in_dim(
+                    back, spare, (val2 + dev_i) % block_out * y1, axis=1
+                )
+        return back
+
     tok_dev = residual.shape[1]
     tok_count = lax.axis_size("tok")
     lat_count = lax.axis_size("lat")
@@ -64,7 +89,7 @@
         ).astype(jnp.bfloat16)
 
     full_delta, full_grad = (
-        lax.all_gather(delta_rows, "lat", axis=1, tiled=True),
+        _meet_clusters(delta_rows),
         lax.all_gather(kl_grad, "lat", axis=1, tiled=True),
     )
     full_width = full_delta.shape[1]

time: 149 us -> 140 us (0.940)
  waiting for transfers between devices: 86.7 us -> 75.1 us
  starting transfers between devices: 13.4 us -> 18 us
    all_gather x1 -> x0, waiting for transfers between devices: 28.2 us -> none  [shards(): lax.all_gather(delta_rows, 'lat', axis=1, tiled=True)]
    ppermute x0 -> x3, waiting for transfers between devices: none -> 16.5 us  [the longest x2 11.6 us: _meet_clusters(): lax.ppermute(upper, link_axis, tuple(((j, (j + 1) % block_out) for j in r...]
    ppermute x0 -> x3, starting transfers between devices: none -> 3.61 us  [the longest x2 2.14 us: _meet_clusters(): lax.ppermute(upper, link_axis, tuple(((j, (j + 1) % block_out) for j in r...]
  transfers between devices with their start and end apart: 8 -> 10, of which waited for: 6 -> 8; matrix products, arithmetic and copies ran while one was open for 7% -> 7% of each run, Pallas kernels for 0% -> 0%
where the time goes in v1:
time: 140 us
  waiting for transfers between devices  75.1 us (54%)
  starting transfers between devices  18 us (13%)
  blocking collectives  16.5 us (12%)
  between operations  13.9 us (10%)
  local copies, waits for them, and re-layouts  5.8 us (4%)
  matrix products  5.52 us (4%)
  other arithmetic  5.2 us (4%)
    reduce_scatter x1, waiting for transfers between devices, shards(): lax.psum_scatter(source_sums.astype(jnp.bfloat16), 'lat', scatter_dimensi...  19.6 us
    psum x1, waiting for transfers between devices, shards(): summed = lax.psum(shared, 'pair').astype(jnp.float32)  19.5 us
    all_to_all x1, blocking collectives, shards(): lax.all_to_all(pieces_out, 'tok', split_axis=0, concat_axis=0, tiled=True)  16.5 us
    all_to_all x1, waiting for transfers between devices, shards(): lax.all_to_all(sent_delta, 'tok', split_axis=0, concat_axis=0, tiled=True)  12.9 us
    ppermute x2, waiting for transfers between devices, _meet_clusters(): lax.ppermute(upper, link_axis, tuple(((j, (j + 1) % block_out) for j in r...  11.6 us
    all_to_all x1, starting transfers between devices, shards(): lax.all_to_all(sent_delta, 'tok', split_axis=0, concat_axis=0, tiled=True)  5.67 us
    ppermute x1, starting transfers between devices, passed_along(): return lax.ppermute(x, axis, pairs)  5.11 us
    ppermute x1, waiting for transfers between devices, _meet_clusters(): lax.ppermute(spare, link_axis, tuple(((j, (j - 1) % block_out) for j in r...  4.88 us
  transfers between devices with their start and end apart: 10, of which 8 were waited for; matrix products, arithmetic and copies ran while one was open for 7% of the time, Pallas kernels for 0%

profile of v1, /device:TPU:0, one launch (start us, length us, event | category | flops | bytes accessed | tf_op | source)
XLA Modules:
  0.0 140.0 jit_solution(4096357669691139438)
XLA Ops:
  7.2 5.1 %collective-permute-start = (bf16[128,1024]{1,0:T(8,128)(2,1)}, bf16[128,1024]{1,0:T(8,128)(2,1)S(1)}, u32[]{:S(2)}, u32[]{:S(2)}) collective-permute-start(bf16[128,1024]{1,0:T(8,128)(2,1)} %bitcast.56), channel_id=1, source_target_pairs={{0,1},{1,2},{2,3},{4,5},{5,6},{6,7},{8,9},{9,10},{10,11},{12,13},{... | collective-permute-start | bytes 786440 | tf_op jit(solution)/shard_map/ppermute | solution.py:14
  12.3 0.7 fusion.21
  13.0 0.7 compare_and_fusion
  13.6 4.5 %collective-permute-done = bf16[128,1024]{1,0:T(8,128)(2,1)S(1)} collective-permute-done((bf16[128,1024]{1,0:T(8,128)(2,1)}, bf16[128,1024]{1,0:T(8,128)(2,1)S(1)}, u32[]{:S(2)}, u32[]{:S(2)}) %collective-permute-start) | collective-permute-done | bytes 262176 | tf_op jit(solution)/shard_map/ppermute | solution.py:14
  18.1 1.0 pad_maximum_fusion
  19.1 0.9 gather_fusion
  20.3 1.4 %collective-permute-done.1 = bf16[128,1024]{1,0:T(8,128)(2,1)S(1)} collective-permute-done((bf16[128,1024]{1,0:T(8,128)(2,1)S(1)}, bf16[128,1024]{1,0:T(8,128)(2,1)S(1)}, u32[]{:S(2)}, u32[]{:S(2)}) %collective-permute-start.1) | collective-permute-done | bytes 262176 | tf_op jit(solution)/shard_map/ppermute | solution.py:18
  22.0 1.5 %collective-permute-start.2 = (bf16[128,1024]{1,0:T(8,128)(2,1)S(1)}, bf16[128,1024]{1,0:T(8,128)(2,1)S(1)}, u32[]{:S(2)}, u32[]{:S(2)}) collective-permute-start(bf16[128,1024]{1,0:T(8,128)(2,1)S(1)} %get-tuple-element.3), channel_id=1, source_target_pairs={{0,4},{4,8},{8,12},{12,0},{1,5},{5,9},{9,13},{13,1},{2,6},{6,10},{... | collective-permute-start | bytes 786440 | tf_op jit(solution)/shard_map/ppermute | solution.py:42
  23.8 1.5 %collective-permute-start.3 = (bf16[128,1024]{1,0:T(8,128)(2,1)S(1)}, bf16[128,1024]{1,0:T(8,128)(2,1)S(1)}, u32[]{:S(2)}, u32[]{:S(2)}) collective-permute-start(bf16[128,1024]{1,0:T(8,128)(2,1)S(1)} %get-tuple-element.3), channel_id=1, source_target_pairs={{0,12},{4,0},{8,4},{12,8},{1,13},{5,1},{9,5},{13,9},{2,14},{6,2},{... | collective-permute-start | bytes 786440 | tf_op jit(solution)/shard_map/ppermute | solution.py:49
  25.3 6.9 %collective-permute-done.2 = bf16[128,1024]{1,0:T(8,128)(2,1)S(1)} collective-permute-done((bf16[128,1024]{1,0:T(8,128)(2,1)S(1)}, bf16[128,1024]{1,0:T(8,128)(2,1)S(1)}, u32[]{:S(2)}, u32[]{:S(2)}) %collective-permute-start.2) | collective-permute-done | bytes 262176 | tf_op jit(solution)/shard_map/ppermute | solution.py:42
  32.1 0.6 collective-permute-start.4
  32.9 4.9 %collective-permute-done.3 = bf16[128,1024]{1,0:T(8,128)(2,1)S(1)} collective-permute-done((bf16[128,1024]{1,0:T(8,128)(2,1)S(1)}, bf16[128,1024]{1,0:T(8,128)(2,1)S(1)}, u32[]{:S(2)}, u32[]{:S(2)}) %collective-permute-start.3) | collective-permute-done | bytes 262176 | tf_op jit(solution)/shard_map/ppermute | solution.py:49
  37.8 4.7 %collective-permute-done.4 = bf16[128,1024]{1,0:T(8,128)(2,1)S(1)} collective-permute-done((bf16[128,1024]{1,0:T(8,128)(2,1)S(1)}, bf16[128,1024]{1,0:T(8,128)(2,1)S(1)}, u32[]{:S(2)}, u32[]{:S(2)}) %collective-permute-start.4) | collective-permute-done | bytes 262176 | tf_op jit(solution)/shard_map/ppermute | solution.py:42
  42.6 1.2 convolution_convert_fusion.1
  43.9 1.1 copy.52
  44.9 5.7 %all-to-all-start = ((bf16[4,2,8,4096]{3,2,1,0:T(8,128)(2,1)}), bf16[4,2,8,4096]{3,2,1,0:T(8,128)(2,1)S(1)}, u32[]{:S(2)}, u32[]{:S(2)}) async-start(bf16[4,2,8,4096]{3,2,1,0:T(8,128)(2,1)} %copy.52), calls=%async_computation | async-start | bytes 1048576 | tf_op jit(solution)/shard_map/all_to_all | solution.py:99
  50.6 0.7 all-gather.2.cloned.1.call-update
  51.7 12.9 %all-to-all-done = bf16[4,2,8,4096]{3,2,1,0:T(8,128)(2,1)S(1)} async-done(((bf16[4,2,8,4096]{3,2,1,0:T(8,128)(2,1)}), bf16[4,2,8,4096]{3,2,1,0:T(8,128)(2,1)S(1)}, u32[]{:S(2)}, u32[]{:S(2)}) %all-to-all-start) | async-done | bytes 524320 | tf_op jit(solution)/shard_map/all_to_all | solution.py:99
  64.6 0.3 fusion.25
  64.9 0.3 convolution_convert_fusion.2
  65.2 0.5 copy.54
  65.7 16.5 %all_to_all.15 = bf16[4,2,8,4096]{3,1,2,0:T(2,128)(2,1)S(1)} all-to-all(bf16[4,2,8,4096]{3,1,2,0:T(2,128)(2,1)S(1)} %copy.54), channel_id=1, replica_groups=mesh['pair'=2,'lat'=4,'tok'=4] {'tok'}, dimensions={0} | all-to-all | bytes 1048576 | tf_op jit(solution)/shard_map/all_to_all | solution.py:117
  82.2 0.7 fusion
  82.9 1.6 %copy.76 = bf16[16,8,4096]{2,1,0:T(8,128)(2,1)} copy(bf16[16,8,4096]{2,0,1:T(8,128)(2,1)S(1)} %fusion) | data formatting | bytes 2097152 | tf_op jit(solution)/shard_map/convert_element_type | solution.py:122
  84.6 2.5 %convolution_convert_fusion = bf16[4,2,8,4096]{3,0,2,1:T(4,128)(2,1)S(1)} fusion(bf16[16,8,4096]{2,1,0:T(8,128)(2,1)} %bitcast.55, s32[4,16]{1,0:T(4,128)S(1)} %copy.50, s32[4,16]{1,0:T(4,128)S(1)} %copy.49), kind=kOutput, calls=%fused_computation.3 | convolution fusion | flops 8651136 | bytes 1573376 | tf_op jit(solution)/shard_map/ksb,btd->kstd/dot_general | solution.py:87
  87.0 1.1 copy.58
  88.1 3.5 %all-to-all-start.2 = ((bf16[4,2,8,4096]{3,2,1,0:T(8,128)(2,1)}), bf16[4,2,8,4096]{3,2,1,0:T(8,128)(2,1)S(1)}, u32[]{:S(2)}, u32[]{:S(2)}) async-start(bf16[4,2,8,4096]{3,2,1,0:T(8,128)(2,1)} %copy.58), calls=%async_computation.3 | async-start | bytes 1048576 | tf_op jit(solution)/shard_map/all_to_all | solution.py:100
  91.7 19.6 %reduce-scatter.2.cloned.1.call-done = bf16[128,1024]{1,0:T(8,128)(2,1)} async-done(((bf16[128,4096]{1,0:T(8,128)(2,1)}), bf16[128,1024]{1,0:T(8,128)(2,1)}) %reduce-scatter.2.cloned.1.call-update) | async-done | bytes 262160 | tf_op jit(solution)/shard_map/reduce_scatter | solution.py:121
  111.3 0.5 fusion.3
  111.7 0.5 broadcast_multiply_fusion
  112.3 19.5 %all-reduce.2.cloned.1.call-done = bf16[128,1024]{1,0:T(8,128)(2,1)} async-done(((bf16[128,1024]{1,0:T(8,128)(2,1)}), bf16[128,1024]{1,0:T(8,128)(2,1)}) %all-reduce.2.cloned.1.call-update) | async-done | bytes 262160 | tf_op jit(solution)/shard_map/psum | solution.py:124
  131.8 1.7 %add_convert_fusion = bf16[128,1024]{1,0:T(8,128)(2,1)} fusion(bf16[128,1024]{1,0:T(8,128)(2,1)} %all-reduce.2.cloned.1.call-done, f32[1024]{0:T(1024)S(1)} %copy-done.2), kind=kLoop, calls=%fused_computation.21 | loop fusion | flops 393216 | bytes 528384 | tf_op jit(solution)/shard_map/convert_element_type | solution.py:125
  (39 shorter events, 1.5 us)
Async XLA Ops:
  7.2 57.7 %copy-start = (bf16[128,4096]{1,0:T(8,128)(2,1)S(1)}, bf16[128,4096]{1,0:T(8,128)(2,1)}, u32[]{:S(2)}) copy-start(bf16[128,4096]{1,0:T(8,128)(2,1)} %param.14) | copy-start | bytes 3145732
  7.2 11.0 %collective-permute-start = (bf16[128,1024]{1,0:T(8,128)(2,1)}, bf16[128,1024]{1,0:T(8,128)(2,1)S(1)}, u32[]{:S(2)}, u32[]{:S(2)}) collective-permute-start(bf16[128,1024]{1,0:T(8,128)(2,1)} %bitcast.56), channel_id=1, source_target_pairs={{0,1},{1,2},{2,3},{4,5},{5,6},{6,7},{8,9},{9,10},{10,11},{12,13},{... | collective-permute-start | bytes 786440 | tf_op jit(solution)/shard_map/ppermute | solution.py:14
  19.1 1.1 copy-start.3
  20.1 1.6 %collective-permute-start.1 = (bf16[128,1024]{1,0:T(8,128)(2,1)S(1)}, bf16[128,1024]{1,0:T(8,128)(2,1)S(1)}, u32[]{:S(2)}, u32[]{:S(2)}) collective-permute-start(bf16[128,1024]{1,0:T(8,128)(2,1)S(1)} %broadcast_select_fusion), channel_id=1, source_target_pairs={{0,16},{16,0},{1,17},{17,1},{2,18},{18,2},{3,19},{19,3},{4,20},{20... | collective-permute-start | bytes 786440 | tf_op jit(solution)/shard_map/ppermute | solution.py:18
  22.0 10.1 %collective-permute-start.2 = (bf16[128,1024]{1,0:T(8,128)(2,1)S(1)}, bf16[128,1024]{1,0:T(8,128)(2,1)S(1)}, u32[]{:S(2)}, u32[]{:S(2)}) collective-permute-start(bf16[128,1024]{1,0:T(8,128)(2,1)S(1)} %get-tuple-element.3), channel_id=1, source_target_pairs={{0,4},{4,8},{8,12},{12,0},{1,5},{5,9},{9,13},{13,1},{2,6},{6,10},{... | collective-permute-start | bytes 786440 | tf_op jit(solution)/shard_map/ppermute | solution.py:42
  23.8 14.0 %collective-permute-start.3 = (bf16[128,1024]{1,0:T(8,128)(2,1)S(1)}, bf16[128,1024]{1,0:T(8,128)(2,1)S(1)}, u32[]{:S(2)}, u32[]{:S(2)}) collective-permute-start(bf16[128,1024]{1,0:T(8,128)(2,1)S(1)} %get-tuple-element.3), channel_id=1, source_target_pairs={{0,12},{4,0},{8,4},{12,8},{1,13},{5,1},{9,5},{13,9},{2,14},{6,2},{... | collective-permute-start | bytes 786440 | tf_op jit(solution)/shard_map/ppermute | solution.py:49
  32.1 10.4 %collective-permute-start.4 = (bf16[128,1024]{1,0:T(8,128)(2,1)S(1)}, bf16[128,1024]{1,0:T(8,128)(2,1)S(1)}, u32[]{:S(2)}, u32[]{:S(2)}) collective-permute-start(bf16[128,1024]{1,0:T(8,128)(2,1)S(1)} %collective-permute-done.2), channel_id=1, source_target_pairs={{0,4},{4,8},{8,12},{12,0},{1,5},{5,9},{9,13},{13,1},{2,6},{6,10},{... | collective-permute-start | bytes 786440 | tf_op jit(solution)/shard_map/ppermute | solution.py:42
  43.8 20.7 %copy-start.1 = (bf16[4096,128]{1,0:T(8,128)(2,1)S(1)}, bf16[4096,128]{1,0:T(8,128)(2,1)}, u32[]{:S(2)}) copy-start(bf16[4096,128]{1,0:T(8,128)(2,1)} %param.12) | copy-start | bytes 3145732
  43.8 20.7 %copy-start.4 = (f32[128]{0:T(128)S(1)}, f32[128]{0:T(128)}, u32[]{:S(2)}) copy-start(f32[128]{0:T(128)} %param.13) | copy-start | bytes 1540
  44.9 19.6 %all-to-all-start = ((bf16[4,2,8,4096]{3,2,1,0:T(8,128)(2,1)}), bf16[4,2,8,4096]{3,2,1,0:T(8,128)(2,1)S(1)}, u32[]{:S(2)}, u32[]{:S(2)}) async-start(bf16[4,2,8,4096]{3,2,1,0:T(8,128)(2,1)} %copy.52), calls=%async_computation | async-start | bytes 1048576 | tf_op jit(solution)/shard_map/all_to_all | solution.py:99
  50.6 33.9 %all-gather.2.cloned.1.call-start = ((), (), s32[]{:S(2)}) async-start(), calls=%async_computation.6 | async-start | bytes 1310720 | tf_op jit(solution)/shard_map/all_gather | solution.py:93
  51.3 59.9 %reduce-scatter.2.cloned.1.call-start = ((), (), s32[]{:S(2)}) async-start(), calls=%async_computation.4 | async-start | bytes 1310720 | tf_op jit(solution)/shard_map/reduce_scatter | solution.py:121
  88.1 23.1 %all-to-all-start.2 = ((bf16[4,2,8,4096]{3,2,1,0:T(8,128)(2,1)}), bf16[4,2,8,4096]{3,2,1,0:T(8,128)(2,1)S(1)}, u32[]{:S(2)}, u32[]{:S(2)}) async-start(bf16[4,2,8,4096]{3,2,1,0:T(8,128)(2,1)} %copy.58), calls=%async_computation.3 | async-start | bytes 1048576 | tf_op jit(solution)/shard_map/all_to_all | solution.py:100
  91.6 40.2 %copy-start.2 = (f32[1024]{0:T(1024)S(1)}, f32[1024]{0:T(1024)}, u32[]{:S(2)}) copy-start(f32[1024]{0:T(1024)} %param.15) | copy-start | bytes 12292
  91.6 40.2 %all-reduce.2.cloned.1.call-start = ((), (), s32[]{:S(2)}) async-start(), calls=%async_computation.5 | async-start | bytes 524288 | tf_op jit(solution)/shard_map/psum | solution.py:124
Sparse Core Ops, SparseCore 0:
  53.3 27.0 all-gather.1
  84.7 26.5 reduce-scatter.1
  113.5 18.2 all-reduce.1
